TPU v7x, 512 devices: a whole 4x8x8 slice. The times are simulated.
512 devices in a mesh: grp: 8 (over z), own: 64 (over y, x, core).
Axes of the slice: x: 4, y: 8, z: 8, core: 2. Of those that a mesh axis runs over, the one named last changes fastest.
Arguments:
- amps: bfloat16 [14336, 128, 128], P(('grp', 'own')), may hold values from -0.35 to 0.35, as said below
- ints: bfloat16 [14336, 128, 128], P(('grp', 'own')), may hold values from -0.5 to 0.5, as said below
- pno_energy: float32 [14336, 128], P(('grp', 'own')), may hold values from 0.2 to 2, as said below
- occ_energy: float32 [1000], replicated, may hold values from -1 to -0.2
- pair_occ: int32 [2, 14336], P(None, ('grp', 'own')), may hold values from 0 to 999, as said below
- mirror: int32 [14336], P(('grp', 'own')), may hold values from 0 to 14335, as said below
- edge_src: int32 [24576], P(('grp', 'own')), may hold values from 0 to 14335, as said below
- edge_dst: int32 [24576], P('grp'), may hold values from 0 to 14335, as said below
- edge_fock: float32 [24576], P(('grp', 'own')), may hold values from -6 to 6
- margin: bfloat16 [24576, 128, 128], P(('grp', 'own')), may hold values from -0.15 to 1.15
Outputs:
- residual: bfloat16 [14336, 128, 128], P(('grp', 'own'))
Inputs may be any that keep to these rules, and one draw needn't show every extreme that they name: `pair_occ`: each pair's two indices differ. The pair at mirror[p] has its two indices swapped. mirror is an involution without fixed points; a pair and its mirror lie in the same grp block of pairs but never on the same device; amps and ints of mirror[p] are the transposes of those of p, and pno_energy is equal. Of one device's pairs at most 1 have their mirror on any one other device, and that many do for some device. `edge_src`: every edge of a device has its source pair on that same device. `edge_dst`: an edge's target pair lies in the same group as its source, on another device; of one device's edges at most 1 end on pairs of any one other device, and at most 1 have the mirror of their target pair on any one device (that device itself included); both bounds are reached on some device. `amps`: mirror pairs hold transposed tiles. `ints`: mirror pairs hold transposed tiles. `pno_energy`: mirror pairs hold equal rows.
All inputs are finite; a program needn't handle non-finite values.
Results may differ from a plain program's by a relative error of at most 0.0065.
Values may be sent and summed in bfloat16 or wider, within the bound.
No kernel may reach another device: no remote copies, remote signals or barrier semaphores. Data moves between devices by JAX's collectives and lax.ppermute only.
A program may use at most 64 MiB of HBM per device.

v0:
```python
import jax
import jax.numpy as jnp
from jax import lax
from jax.sharding import PartitionSpec as P


def rank_within(targets, buckets):
    onehot = (targets[:, None] == lax.iota(jnp.int32, buckets)[None, :]).astype(jnp.int32)
    running = jnp.cumsum(onehot, axis=0)
    return jnp.sum(onehot * running, axis=1) - 1


def pick_rows(lookup, hit_mask):
    return jnp.sum(jnp.where(hit_mask, lookup[None, :], 0.0), axis=1)


def pack_tiles(tile_set, targets, owners, capacity):
    placed = targets * capacity + rank_within(targets, owners)
    blank_buffer = jnp.zeros((owners * capacity,) + tile_set.shape[1:], tile_set.dtype)
    return blank_buffer.at[placed].set(tile_set)


def arrival_sum(arrived, destination, row_ids, row_total, owners, capacity, my_owner):
    per_sender = destination.shape[0] // owners
    arriving = destination == my_owner
    sender = lax.iota(jnp.int32, owners * per_sender) // per_sender
    counted = (
        jnp.cumsum(arriving.reshape(owners, per_sender).astype(jnp.int32), axis=1).reshape(-1) - 1
    )
    column = sender * capacity + counted
    row_hit = (
        (row_ids[:, None] == lax.iota(jnp.int32, row_total)[None, :]) & arriving[:, None]
    ).astype(jnp.float32)
    column_hit = (column[:, None] == lax.iota(jnp.int32, owners * capacity)[None, :]).astype(
        jnp.float32
    )
    selector = jnp.dot(row_hit.T, column_hit).astype(jnp.bfloat16)
    tile_rows = arrived.shape[1]
    tile_cols = arrived.shape[2]
    summed = jnp.dot(
        selector,
        arrived.reshape(owners * capacity, tile_rows * tile_cols),
        preferred_element_type=jnp.float32,
    )
    return summed.reshape(row_total, tile_rows, tile_cols)


def local(
    amps, ints, pno_energy, occ_energy, pair_occ, mirror, edge_src, edge_dst, edge_fock, margin
):
    owners = lax.axis_size("own")
    my_owner = lax.axis_index("own")
    group_index = lax.axis_index("grp")
    per_device = amps.shape[0]
    pno_rank = amps.shape[1]
    edge_count = edge_src.shape[0]
    occ_count = occ_energy.shape[0]
    mirror_cap = (per_device + owners - 2) // (owners - 1)
    edge_cap = (edge_count + owners - 2) // (owners - 1)
    group_base = group_index * (owners * per_device)
    device_base = group_base + my_owner * per_device
    amp_f32 = amps.astype(jnp.float32)
    int_f32 = ints.astype(jnp.float32)
    pair_energy = jnp.sum((2.0 * int_f32 - jnp.swapaxes(int_f32, 1, 2)) * amp_f32, axis=(1, 2))
    occ_ids = lax.iota(jnp.int32, occ_count)
    first_hit = pair_occ[0][:, None] == occ_ids[None, :]
    second_hit = pair_occ[1][:, None] == occ_ids[None, :]
    partial_value = jnp.sum(jnp.where(first_hit, pair_energy[:, None], 0.0), axis=0)
    source_local = edge_src - device_base
    source_tiles = jnp.take(amps, source_local, axis=0)
    projected = jnp.einsum(
        "eab,ebc->eac", margin, source_tiles, preferred_element_type=jnp.float32
    ).astype(jnp.bfloat16)
    product = jnp.einsum("eab,ecb->eac", projected, margin, preferred_element_type=jnp.float32)
    coupled = (product * edge_fock[:, None, None]).astype(jnp.bfloat16)
    group_dst = edge_dst - group_base
    dst_owner = group_dst // per_device
    dst_slot = group_dst % per_device
    my_dst_owner = lax.dynamic_slice_in_dim(dst_owner, my_owner * edge_count, edge_count)
    mirror_local = mirror - group_base
    mirror_owner = mirror_local // per_device
    mirror_slot = mirror_local % per_device
    slot_ids = lax.iota(jnp.int32, per_device)
    same_owner = mirror_owner[:, None] == mirror_owner[None, :]
    out_rank = jnp.sum(same_owner & (slot_ids[None, :] < slot_ids[:, None]), axis=1)
    in_rank = jnp.sum(same_owner & (mirror_slot[None, :] < mirror_slot[:, None]), axis=1)
    out_place = mirror_owner * mirror_cap + out_rank
    in_place = mirror_owner * mirror_cap + in_rank
    outgoing = pack_tiles(coupled, my_dst_owner, owners, edge_cap)
    arrived = lax.all_to_all(outgoing, "own", split_axis=0, concat_axis=0, tiled=True)
    coupling = arrival_sum(arrived, dst_owner, dst_slot, per_device, owners, edge_cap, my_owner)
    occ_sums = lax.psum(partial_value, ("grp", "own"))
    cepa_shift = 0.5 * (pick_rows(occ_sums, first_hit) + pick_rows(occ_sums, second_hit))
    fock_pair = pick_rows(occ_energy, first_hit) + pick_rows(occ_energy, second_hit)
    diagonal = (
        pno_energy[:, :, None]
        + pno_energy[:, None, :]
        - fock_pair[:, None, None]
        - cepa_shift[:, None, None]
    )
    local_part = 0.5 * int_f32 + diagonal * amp_f32
    half_res = (local_part + coupling).astype(jnp.bfloat16)
    sent_tiles = (
        jnp.zeros((owners * mirror_cap, pno_rank, pno_rank), jnp.bfloat16)
        .at[out_place]
        .set(half_res)
    )
    returned = lax.all_to_all(sent_tiles, "own", split_axis=0, concat_axis=0, tiled=True)
    partner_tiles = jnp.swapaxes(jnp.take(returned, in_place, axis=0), 1, 2)
    return (half_res.astype(jnp.float32) + partner_tiles.astype(jnp.float32)).astype(jnp.bfloat16)


def solution(mesh):
    in_specs = (
        P(("grp", "own"), None, None),
        P(("grp", "own"), None, None),
        P(("grp", "own"), None),
        P(),
        P(None, ("grp", "own")),
        P(("grp", "own")),
        P(("grp", "own")),
        P("grp"),
        P(("grp", "own")),
        P(("grp", "own"), None, None),
    )
    out_specs = P(("grp", "own"), None, None)
    return jax.shard_map(local, mesh=mesh, in_specs=in_specs, out_specs=out_specs, check_vma=False)
```

profile of v0, /device:TPU:2, one launch (start us, length us, event | category | flops | bytes accessed | tf_op | source)
XLA Modules:
  0.0 255.8 jit_solution(17630321323486701804)
XLA Ops:
  0.0 0.0 copy-start
  0.0 0.8 fusion.33
  0.9 0.1 dynamic_slice.3
  0.9 0.1 fusion.25
  1.0 0.1 reduce_window_sum.23
  1.1 0.2 select_reduce_fusion.5
  1.3 0.1 compare_select_fusion.3
  1.4 0.7 compare_and_fusion.3
  2.0 3.1 %gather_fusion = bf16[48,128,128]{2,1,0:T(8,128)(2,1)} fusion(bf16[28,128,128]{2,1,0:T(8,128)(2,1)} %param.10, s32[1024]{0:T(1024)S(1)} %pad_clamp_fusion.1), kind=kCustom, calls=%fused_computation | custom fusion | bytes 3145920 | tf_op jit(solution)/shard_map/jit(_take)/gather | solution.py:70
  5.2 0.0 copy-done
  5.2 0.0 copy-done.8
  5.2 3.7 %multiply_convert_fusion = bf16[48,128,128]{2,1,0:T(8,128)(2,1)S(1)} fusion(bf16[48,128,128]{2,1,0:T(8,128)(2,1)S(1)} %copy-done, f32[48]{0:T(128)S(1)} %copy-done.8, bf16[48,128,128]{2,1,0:T(8,128)(2,1)} %gather_fusion, pred[48]{0:T(512)(128)(4,1)S(1)} %get-tuple-element.18), kind=kOutput, calls=%fused_computation.4 | convolution fusion | flops 405798912 | bytes 4718832 | tf_op jit(solution)/shard_map/eab,ecb->eac/dot_general | solution.py:74
  8.9 1.8 broadcast.97.clone
  10.7 6.6 %scatter_fusion = bf16[64,128,128]{2,1,0:T(8,128)(2,1)} fusion(bf16[64,128,128]{2,1,0:T(8,128)(2,1)} %broadcast.97.clone, s32[48]{0:T(128)S(1)} %compare_select_fusion.3, bf16[48,128,128]{2,1,0:T(8,128)(2,1)S(1)} %multiply_convert_fusion), kind=kCustom, calls=%fused_computation.2 | custom fusion | bytes 4718784 | tf_op jit(solution)/shard_map/scatter | solution.py:20
  17.3 11.0 %all-to-all-start = ((bf16[64,128,128]{2,1,0:T(8,128)(2,1)}), bf16[64,128,128]{2,1,0:T(8,128)(2,1)}, u32[]{:S(2)}, u32[]{:S(2)}) async-start(bf16[64,128,128]{2,1,0:T(8,128)(2,1)} %scatter_fusion), calls=%async_computation | async-start | bytes 4194304 | tf_op jit(solution)/shard_map/all_to_all | solution.py:90
  28.3 0.0 copy-done.2
  28.3 1.3 copy.39
  29.6 0.1 reshape.67
  29.6 0.2 reduce_window_sum.22
  29.9 0.1 sub.71
  30.0 1.5 copy.37
  31.4 0.0 copy-done.6
  31.4 0.0 copy-start.5
  31.5 0.0 copy-start.7
  31.5 0.0 copy-start.4
  31.5 2.0 fusion.3
  33.5 0.1 select_reduce_fusion.2
  33.6 137.7 %psum.7 = f32[1000]{0:T(1024)S(1)} all-reduce(f32[1000]{0:T(1024)S(1)} %select_reduce_fusion.2), channel_id=1, replica_groups=mesh['grp'=8,'own'=64] {'grp','own'}, use_global_device_ids=true, to_apply=%region_4.5 | all-reduce | flops 1000 | bytes 8000 | tf_op jit(solution)/shard_map/psum | solution.py:92
  171.3 0.0 copy-done.5
  171.3 0.3 select_reduce_fusion
  171.6 0.0 copy-done.7
  171.6 0.2 convert_reduce_fusion.1
  171.8 0.0 copy-done.4
  171.9 0.0 all-to-all-done
  171.9 4.9 %fusion = f32[28,128,128]{2,0,1:T(8,128)} fusion(s32[3072]{0:T(1024)S(1)} %get-tuple-element.25, s32[3072]{0:T(1024)S(1)} %get-tuple-element.24, pred[3072]{0:T(1024)(128)(4,1)S(1)} %get-tuple-element.16, bf16[8,8,128,128]{3,2,1,0:T(8,128)(2,1)} %bitcast.8), kind=kOutput, calls=%fused_computation.8 | convolution fusion | flops 70100736 | bytes 3959808 | tf_op jit(solution)/shard_map/dot_general | solution.py:40
  176.8 2.9 %copy.43 = f32[28,128,128]{1,2,0:T(8,128)} copy(f32[28,128,128]{2,0,1:T(8,128)} %fusion) | data formatting | bytes 3670016 | tf_op jit(solution)/shard_map/dot_general | solution.py:40
  179.7 0.0 copy-done.3
  179.7 3.1 %fusion.6 = bf16[28,128,128]{1,2,0:T(8,128)(2,1)} fusion(f32[28,128,128]{1,2,0:T(8,128)} %copy.43, bf16[28,128,128]{1,2,0:T(8,128)(2,1)} %copy.39, f32[28,128,128]{1,2,0:T(8,128)S(1)} %copy.37, f32[28]{0:T(128)S(1)} %add_multiply_fusion, f32[28]{0:T(128)S(1)} %add.110, f32[28,128]{1,0:T(8,128)S(1)} %copy-done.3), kind=kLoop, calls=%fused_computation.14 | loop fusion | flops 4128768 | bytes 5519584 | tf_op jit(solution)/shard_map/convert_element_type | solution.py:102
  182.8 1.6 copy.44
  184.4 1.8 broadcast.97
  186.2 4.5 %scatter_fusion.1 = bf16[64,128,128]{2,1,0:T(8,128)(2,1)} fusion(bf16[64,128,128]{2,1,0:T(8,128)(2,1)} %broadcast.97, s32[28]{0:T(128)S(1)} %compare_select_fusion, bf16[28,128,128]{2,1,0:T(8,128)(2,1)S(1)} %copy.44), kind=kCustom, calls=%fused_computation.3 | custom fusion | bytes 2752624 | tf_op jit(solution)/shard_map/scatter | solution.py:106
  190.7 7.8 %all-to-all-start.1 = ((bf16[64,128,128]{2,1,0:T(8,128)(2,1)}), bf16[64,128,128]{2,1,0:T(8,128)(2,1)}, u32[]{:S(2)}, u32[]{:S(2)}) async-start(bf16[64,128,128]{2,1,0:T(8,128)(2,1)} %scatter_fusion.1), calls=%async_computation.1 | async-start | bytes 4194304 | tf_op jit(solution)/shard_map/all_to_all | solution.py:108
  198.5 0.0 copy-start.1
  198.6 51.1 %all-to-all-done.1 = bf16[64,128,128]{2,1,0:T(8,128)(2,1)} async-done(((bf16[64,128,128]{2,1,0:T(8,128)(2,1)}), bf16[64,128,128]{2,1,0:T(8,128)(2,1)}, u32[]{:S(2)}, u32[]{:S(2)}) %all-to-all-start.1) | async-done | bytes 2097184 | tf_op jit(solution)/shard_map/all_to_all | solution.py:108
  249.7 3.2 %gather_fusion.1 = bf16[28,128,128]{2,1,0:T(8,128)(2,1)} fusion(bf16[64,128,128]{2,1,0:T(8,128)(2,1)} %all-to-all-done.1, s32[1024]{0:T(1024)S(1)} %pad_clamp_fusion), kind=kCustom, calls=%fused_computation.1 | custom fusion | bytes 1835120 | tf_op jit(solution)/shard_map/jit(_take)/gather | solution.py:109
  252.9 0.0 copy-done.1
  252.9 1.6 fusion.7
  254.5 1.3 copy.45
  (14 shorter events, 0.1 us)
Async XLA Ops:
  0.0 5.2 %copy-start = (bf16[48,128,128]{2,1,0:T(8,128)(2,1)S(1)}, bf16[48,128,128]{2,1,0:T(8,128)(2,1)}, u32[]{:S(2)}) copy-start(bf16[48,128,128]{2,1,0:T(8,128)(2,1)} %param.19) | copy-start | bytes 4718596
  0.0 5.2 %copy-start.8 = (f32[48]{0:T(128)S(1)}, f32[48]{0:T(128)}, u32[]{:S(2)}) copy-start(f32[48]{0:T(128)} %param.18) | copy-start | bytes 580
  17.3 11.0 %copy-start.2 = (bf16[28,128,128]{2,1,0:T(8,128)(2,1)S(1)}, bf16[28,128,128]{2,1,0:T(8,128)(2,1)}, u32[]{:S(2)}) copy-start(bf16[28,128,128]{2,1,0:T(8,128)(2,1)} %param.10) | copy-start | bytes 2752516
  17.3 154.6 %all-to-all-start = ((bf16[64,128,128]{2,1,0:T(8,128)(2,1)}), bf16[64,128,128]{2,1,0:T(8,128)(2,1)}, u32[]{:S(2)}, u32[]{:S(2)}) async-start(bf16[64,128,128]{2,1,0:T(8,128)(2,1)} %scatter_fusion), calls=%async_computation | async-start | bytes 4194304 | tf_op jit(solution)/shard_map/all_to_all | solution.py:90
  29.6 1.8 copy-start.6
  31.4 139.9 %copy-start.5 = (f32[1000]{0:T(1024)S(1)}, f32[1000]{0:T(1024)}, u32[]{:S(2)}) copy-start(f32[1000]{0:T(1024)} %param.13) | copy-start | bytes 12004
  31.5 140.2 %copy-start.7 = (s32[28]{0:T(128)S(1)}, s32[28]{0:T(128)}, u32[]{:S(2)}) copy-start(s32[28]{0:T(128)} %param.15) | copy-start | bytes 340
  31.5 140.4 %copy-start.4 = (s32[3072]{0:T(1024)S(1)}, s32[3072]{0:T(1024)}, u32[]{:S(2)}) copy-start(s32[3072]{0:T(1024)} %param.17) | copy-start | bytes 36868
  176.8 2.9 %copy-start.3 = (f32[28,128]{1,0:T(8,128)S(1)}, f32[28,128]{1,0:T(8,128)}, u32[]{:S(2)}) copy-start(f32[28,128]{1,0:T(8,128)} %param.12) | copy-start | bytes 43012
  190.7 59.0 %all-to-all-start.1 = ((bf16[64,128,128]{2,1,0:T(8,128)(2,1)}), bf16[64,128,128]{2,1,0:T(8,128)(2,1)}, u32[]{:S(2)}, u32[]{:S(2)}) async-start(bf16[64,128,128]{2,1,0:T(8,128)(2,1)} %scatter_fusion.1), calls=%async_computation.1 | async-start | bytes 4194304 | tf_op jit(solution)/shard_map/all_to_all | solution.py:108
  198.5 54.4 %copy-start.1 = (bf16[28,128,128]{1,2,0:T(8,128)(2,1)S(1)}, bf16[28,128,128]{1,2,0:T(8,128)(2,1)}, u32[]{:S(2)}) copy-start(bf16[28,128,128]{1,2,0:T(8,128)(2,1)} %fusion.6) | copy-start | bytes 2752516
where the time goes:
time: 257 us; the launch traced here: 256 us
  blocking collectives  138 us (54%)
  waiting for transfers between devices  51.1 us (20%)
  local copies, waits for them, and re-layouts  29.9 us (12%)
  starting transfers between devices  18.8 us (7%)
  other arithmetic  9.49 us (4%)
  matrix products  8.65 us (3%)
    psum x1, blocking collectives, local(): occ_sums = lax.psum(partial_value, ('grp', 'own'))  138 us
    all_to_all x1, waiting for transfers between devices, local(): lax.all_to_all(sent_tiles, 'own', split_axis=0, concat_axis=0, tiled=True)  51.1 us
    all_to_all x1, starting transfers between devices, local(): lax.all_to_all(outgoing, 'own', split_axis=0, concat_axis=0, tiled=True)  11 us
    all_to_all x1, starting transfers between devices, local(): lax.all_to_all(sent_tiles, 'own', split_axis=0, concat_axis=0, tiled=True)  7.79 us
    scatter x1, local copies, waits for them, and re-layouts, pack_tiles(): return blank_buffer.at[placed].set(tile_set)  6.61 us
  transfers between devices with their start and end apart: 2, of which 1 were waited for; matrix products, arithmetic and copies ran while one was open for 2% of the time, Pallas kernels for 0%

commit v1 on v0

--- a/solution.py
+++ b/solution.py
@@ -89,7 +89,7 @@
     outgoing = pack_tiles(coupled, my_dst_owner, owners, edge_cap)
     arrived = lax.all_to_all(outgoing, "own", split_axis=0, concat_axis=0, tiled=True)
     coupling = arrival_sum(arrived, dst_owner, dst_slot, per_device, owners, edge_cap, my_owner)
-    occ_sums = lax.psum(partial_value, ("grp", "own"))
+    occ_sums = lax.psum(lax.psum(partial_value, "own"), "grp")
     cepa_shift = 0.5 * (pick_rows(occ_sums, first_hit) + pick_rows(occ_sums, second_hit))
     fock_pair = pick_rows(occ_energy, first_hit) + pick_rows(occ_energy, second_hit)
     diagonal = (

time: 257 us -> 304 us (1.18)
  blocking collectives: 138 us -> 178 us
  starting transfers between devices: 18.8 us -> 25.6 us
    psum x1 -> x2, blocking collectives: 138 us -> 178 us  [local(): occ_sums = lax.psum(lax.psum(partial_value, 'own'), 'grp')]
    all_to_all x1, starting transfers between devices: 7.79 us -> 14.7 us  [local(): lax.all_to_all(sent_tiles, 'own', split_axis=0, concat_axis=0, tiled=True)]
where the time goes in v1:
time: 304 us; the launch traced here: 303 us
  blocking collectives  178 us (59%)
  waiting for transfers between devices  51.1 us (17%)
  local copies, waits for them, and re-layouts  29.9 us (10%)
  starting transfers between devices  25.6 us (8%)
  other arithmetic  9.49 us (3%)
  matrix products  8.65 us (3%)
    psum x2, blocking collectives, local(): occ_sums = lax.psum(lax.psum(partial_value, 'own'), 'grp')  178 us
    all_to_all x1, waiting for transfers between devices, local(): lax.all_to_all(sent_tiles, 'own', split_axis=0, concat_axis=0, tiled=True)  51.1 us
    all_to_all x1, starting transfers between devices, local(): lax.all_to_all(sent_tiles, 'own', split_axis=0, concat_axis=0, tiled=True)  14.7 us
    all_to_all x1, starting transfers between devices, local(): lax.all_to_all(outgoing, 'own', split_axis=0, concat_axis=0, tiled=True)  11 us
    scatter x1, local copies, waits for them, and re-layouts, pack_tiles(): return blank_buffer.at[placed].set(tile_set)  6.61 us
  transfers between devices with their start and end apart: 2, of which 1 were waited for; matrix products, arithmetic and copies ran while one was open for 2% of the time, Pallas kernels for 0%

profile of v1, /device:TPU:2, one launch (start us, length us, event | category | flops | bytes accessed | tf_op | source)
XLA Modules:
  0.0 302.8 jit_solution(12922482726758945807)
XLA Ops:
  0.0 0.0 copy-start
  0.0 0.8 fusion.33
  0.9 0.1 dynamic_slice.3
  0.9 0.1 fusion.25
  1.0 0.1 reduce_window_sum.23
  1.1 0.2 select_reduce_fusion.5
  1.3 0.1 compare_select_fusion.3
  1.4 0.7 compare_and_fusion.3
  2.0 3.1 %gather_fusion = bf16[48,128,128]{2,1,0:T(8,128)(2,1)} fusion(bf16[28,128,128]{2,1,0:T(8,128)(2,1)} %param.10, s32[1024]{0:T(1024)S(1)} %pad_clamp_fusion.1), kind=kCustom, calls=%fused_computation | custom fusion | bytes 3145920 | tf_op jit(solution)/shard_map/jit(_take)/gather | solution.py:70
  5.2 0.0 copy-done
  5.2 0.0 copy-done.8
  5.2 3.7 %multiply_convert_fusion = bf16[48,128,128]{2,1,0:T(8,128)(2,1)S(1)} fusion(bf16[48,128,128]{2,1,0:T(8,128)(2,1)S(1)} %copy-done, f32[48]{0:T(128)S(1)} %copy-done.8, bf16[48,128,128]{2,1,0:T(8,128)(2,1)} %gather_fusion, pred[48]{0:T(512)(128)(4,1)S(1)} %get-tuple-element.18), kind=kOutput, calls=%fused_computation.4 | convolution fusion | flops 405798912 | bytes 4718832 | tf_op jit(solution)/shard_map/eab,ecb->eac/dot_general | solution.py:74
  8.9 1.8 broadcast.97.clone
  10.7 6.6 %scatter_fusion = bf16[64,128,128]{2,1,0:T(8,128)(2,1)} fusion(bf16[64,128,128]{2,1,0:T(8,128)(2,1)} %broadcast.97.clone, s32[48]{0:T(128)S(1)} %compare_select_fusion.3, bf16[48,128,128]{2,1,0:T(8,128)(2,1)S(1)} %multiply_convert_fusion), kind=kCustom, calls=%fused_computation.2 | custom fusion | bytes 4718784 | tf_op jit(solution)/shard_map/scatter | solution.py:20
  17.3 11.0 %all-to-all-start = ((bf16[64,128,128]{2,1,0:T(8,128)(2,1)}), bf16[64,128,128]{2,1,0:T(8,128)(2,1)}, u32[]{:S(2)}, u32[]{:S(2)}) async-start(bf16[64,128,128]{2,1,0:T(8,128)(2,1)} %scatter_fusion), calls=%async_computation | async-start | bytes 4194304 | tf_op jit(solution)/shard_map/all_to_all | solution.py:90
  28.3 0.0 copy-done.2
  28.3 1.3 copy.39
  29.6 0.1 reshape.67
  29.6 0.2 reduce_window_sum.22
  29.9 0.1 sub.71
  30.0 1.5 copy.37
  31.4 0.0 copy-done.6
  31.4 0.0 copy-start.5
  31.5 0.0 copy-start.7
  31.5 0.0 copy-start.4
  31.5 2.0 fusion.3
  33.5 0.1 select_reduce_fusion.2
  33.6 154.6 %psum.14 = f32[1000]{0:T(1024)S(1)} all-reduce(f32[1000]{0:T(1024)S(1)} %select_reduce_fusion.2), channel_id=1, replica_groups=mesh['grp'=8,'own'=64] {'own'}, use_global_device_ids=true, to_apply=%region_4.5 | all-reduce | flops 1000 | bytes 8000 | tf_op jit(solution)/shard_map/psum | solution.py:92
  188.2 23.2 %psum.15 = f32[1000]{0:T(1024)S(1)} all-reduce(f32[1000]{0:T(1024)S(1)} %psum.14), channel_id=1, replica_groups=mesh['grp'=8,'own'=64] {'grp'}, use_global_device_ids=true, to_apply=%region_5.6 | all-reduce | flops 1000 | bytes 8000 | tf_op jit(solution)/shard_map/psum | solution.py:92
  211.4 0.0 copy-done.5
  211.4 0.3 select_reduce_fusion
  211.7 0.0 copy-done.7
  211.7 0.2 convert_reduce_fusion.1
  212.0 0.0 all-to-all-done
  212.0 4.9 %fusion = f32[28,128,128]{2,0,1:T(8,128)} fusion(s32[3072]{0:T(1024)S(1)} %get-tuple-element.25, s32[3072]{0:T(1024)S(1)} %get-tuple-element.24, pred[3072]{0:T(1024)(128)(4,1)S(1)} %get-tuple-element.16, bf16[8,8,128,128]{3,2,1,0:T(8,128)(2,1)} %bitcast.8), kind=kOutput, calls=%fused_computation.8 | convolution fusion | flops 70100736 | bytes 3959808 | tf_op jit(solution)/shard_map/dot_general | solution.py:40
  216.9 2.9 copy.43
  219.9 0.0 copy-done.3
  219.9 3.1 %fusion.6 = bf16[28,128,128]{1,2,0:T(8,128)(2,1)} fusion(f32[28,128,128]{1,2,0:T(8,128)} %copy.43, bf16[28,128,128]{1,2,0:T(8,128)(2,1)} %copy.39, f32[28,128,128]{1,2,0:T(8,128)S(1)} %copy.37, f32[28]{0:T(128)S(1)} %add_multiply_fusion, f32[28]{0:T(128)S(1)} %add.112, f32[28,128]{1,0:T(8,128)S(1)} %copy-done.3), kind=kLoop, calls=%fused_computation.14 | loop fusion | flops 4128768 | bytes 5519584 | tf_op jit(solution)/shard_map/convert_element_type | solution.py:102
  222.9 1.6 copy.44
  224.5 1.8 broadcast.97
  226.3 4.5 %scatter_fusion.1 = bf16[64,128,128]{2,1,0:T(8,128)(2,1)} fusion(bf16[64,128,128]{2,1,0:T(8,128)(2,1)} %broadcast.97, s32[28]{0:T(128)S(1)} %compare_select_fusion, bf16[28,128,128]{2,1,0:T(8,128)(2,1)S(1)} %copy.44), kind=kCustom, calls=%fused_computation.3 | custom fusion | bytes 2752624 | tf_op jit(solution)/shard_map/scatter | solution.py:106
  230.8 14.7 %all-to-all-start.1 = ((bf16[64,128,128]{2,1,0:T(8,128)(2,1)}), bf16[64,128,128]{2,1,0:T(8,128)(2,1)}, u32[]{:S(2)}, u32[]{:S(2)}) async-start(bf16[64,128,128]{2,1,0:T(8,128)(2,1)} %scatter_fusion.1), calls=%async_computation.1 | async-start | bytes 4194304 | tf_op jit(solution)/shard_map/all_to_all | solution.py:108
  245.5 0.0 copy-start.1
  245.5 51.1 %all-to-all-done.1 = bf16[64,128,128]{2,1,0:T(8,128)(2,1)} async-done(((bf16[64,128,128]{2,1,0:T(8,128)(2,1)}), bf16[64,128,128]{2,1,0:T(8,128)(2,1)}, u32[]{:S(2)}, u32[]{:S(2)}) %all-to-all-start.1) | async-done | bytes 2097184 | tf_op jit(solution)/shard_map/all_to_all | solution.py:108
  296.7 3.2 %gather_fusion.1 = bf16[28,128,128]{2,1,0:T(8,128)(2,1)} fusion(bf16[64,128,128]{2,1,0:T(8,128)(2,1)} %all-to-all-done.1, s32[1024]{0:T(1024)S(1)} %pad_clamp_fusion), kind=kCustom, calls=%fused_computation.1 | custom fusion | bytes 1835120 | tf_op jit(solution)/shard_map/jit(_take)/gather | solution.py:109
  299.9 0.0 copy-done.1
  299.9 1.6 fusion.7
  301.5 1.3 copy.45
  (15 shorter events, 0.1 us)
Async XLA Ops:
  0.0 5.2 %copy-start = (bf16[48,128,128]{2,1,0:T(8,128)(2,1)S(1)}, bf16[48,128,128]{2,1,0:T(8,128)(2,1)}, u32[]{:S(2)}) copy-start(bf16[48,128,128]{2,1,0:T(8,128)(2,1)} %param.19) | copy-start | bytes 4718596
  0.0 5.2 %copy-start.8 = (f32[48]{0:T(128)S(1)}, f32[48]{0:T(128)}, u32[]{:S(2)}) copy-start(f32[48]{0:T(128)} %param.18) | copy-start | bytes 580
  17.3 11.0 %copy-start.2 = (bf16[28,128,128]{2,1,0:T(8,128)(2,1)S(1)}, bf16[28,128,128]{2,1,0:T(8,128)(2,1)}, u32[]{:S(2)}) copy-start(bf16[28,128,128]{2,1,0:T(8,128)(2,1)} %param.10) | copy-start | bytes 2752516
  17.3 194.7 %all-to-all-start = ((bf16[64,128,128]{2,1,0:T(8,128)(2,1)}), bf16[64,128,128]{2,1,0:T(8,128)(2,1)}, u32[]{:S(2)}, u32[]{:S(2)}) async-start(bf16[64,128,128]{2,1,0:T(8,128)(2,1)} %scatter_fusion), calls=%async_computation | async-start | bytes 4194304 | tf_op jit(solution)/shard_map/all_to_all | solution.py:90
  29.6 1.8 copy-start.6
  31.4 180.0 %copy-start.5 = (f32[1000]{0:T(1024)S(1)}, f32[1000]{0:T(1024)}, u32[]{:S(2)}) copy-start(f32[1000]{0:T(1024)} %param.13) | copy-start | bytes 12004
  31.5 180.3 %copy-start.7 = (s32[28]{0:T(128)S(1)}, s32[28]{0:T(128)}, u32[]{:S(2)}) copy-start(s32[28]{0:T(128)} %param.15) | copy-start | bytes 340
  31.5 180.5 %copy-start.4 = (s32[3072]{0:T(1024)S(1)}, s32[3072]{0:T(1024)}, u32[]{:S(2)}) copy-start(s32[3072]{0:T(1024)} %param.17) | copy-start | bytes 36868
  216.9 2.9 copy-start.3
  230.8 65.8 %all-to-all-start.1 = ((bf16[64,128,128]{2,1,0:T(8,128)(2,1)}), bf16[64,128,128]{2,1,0:T(8,128)(2,1)}, u32[]{:S(2)}, u32[]{:S(2)}) async-start(bf16[64,128,128]{2,1,0:T(8,128)(2,1)} %scatter_fusion.1), calls=%async_computation.1 | async-start | bytes 4194304 | tf_op jit(solution)/shard_map/all_to_all | solution.py:108
  245.5 54.4 %copy-start.1 = (bf16[28,128,128]{1,2,0:T(8,128)(2,1)S(1)}, bf16[28,128,128]{1,2,0:T(8,128)(2,1)}, u32[]{:S(2)}) copy-start(bf16[28,128,128]{1,2,0:T(8,128)(2,1)} %fusion.6) | copy-start | bytes 2752516
